TPU v7x, 32 devices: a whole 2x2x4 slice. The times are simulated.
32 devices in a mesh: row: 4 (over y, core), col: 8 (over z, x).
Axes of the slice: x: 2, y: 2, z: 4, core: 2. Of those that a mesh axis runs over, the one named last changes fastest.
Arguments:
- weight: bfloat16 [8192, 16384], P('row', 'col'), may hold values from -3 to 3
- momentum: float32 [8192, 16384], P('row', 'col'), may hold values from -100 to 100, as said below
- gradient: bfloat16 [8192, 16384], P('row', 'col'), may hold values from -6 to 6
- prev_basis: bfloat16 [16384, 512], P('col'), may hold values from -6 to 6
Outputs:
- new_weight: bfloat16 [8192, 16384], P('row', 'col')
- new_momentum: float32 [8192, 16384], P('row', 'col')
- new_basis: bfloat16 [16384, 512], P('col')
Inputs may be any that keep to these rules, and one draw needn't show every extreme that they name: momentum has rows and columns of different scales.
All inputs are finite; a program needn't handle non-finite values.
Results may differ from a plain program's by a relative error of at most 0.0021.
Values may be sent and summed in bfloat16 or wider, within the bound.
No kernel may reach another device: no remote copies, remote signals or barrier semaphores. Data moves between devices by JAX's collectives and lax.ppermute only.
A program may use at most 128 MiB of HBM per device.

v0:
```python
import jax
import jax.numpy as jnp
from jax import lax
from jax.sharding import PartitionSpec as P

M = 8192
N = 16384
decay_loss = 0.1
step_size = 0.4
epsilon = 1e-06


def orthogonalize(left_factor, gram_matrix):
    lower_tri = jnp.linalg.cholesky(gram_matrix)
    return jax.scipy.linalg.solve_triangular(lower_tri, left_factor.T, lower=True).T


def per_device(weight, momentum, gradient, prev_basis):
    high = lax.Precision.HIGHEST
    buffer = momentum + gradient.astype(jnp.float32)
    partial_left = jnp.dot(buffer, prev_basis.astype(jnp.float32), precision=high)
    left_factor = lax.psum(partial_left, "col")
    gram_matrix = lax.psum(jnp.dot(left_factor.T, left_factor, precision=high), "row")
    orthonormal = orthogonalize(left_factor, gram_matrix)
    right_piece = lax.psum_scatter(
        jnp.dot(buffer.T, orthonormal, precision=high), "row", scatter_dimension=0, tiled=True
    )
    square_sum = lax.psum(jnp.sum(right_piece * right_piece, axis=0), ("row", "col"))
    column_scale = jnp.sqrt(square_sum / N + epsilon)
    basis_piece = (right_piece / column_scale).astype(jnp.bfloat16)
    new_basis = lax.all_gather(basis_piece, "row", axis=0, tiled=True)
    basis_float = new_basis.astype(jnp.float32)
    new_momentum = buffer - decay_loss * jnp.dot(
        orthonormal * column_scale, basis_float.T, precision=high
    )
    update = jnp.dot(orthonormal, basis_float.T, precision=high)
    new_weight = (weight.astype(jnp.float32) - step_size * (M / N) ** 0.5 * update).astype(
        jnp.bfloat16
    )
    return (new_weight, new_momentum, new_basis)


def solution(mesh):
    return jax.shard_map(
        per_device,
        mesh=mesh,
        in_specs=(P("row", "col"), P("row", "col"), P("row", "col"), P("col", None)),
        out_specs=(P("row", "col"), P("row", "col"), P("col", None)),
        check_vma=False,
    )
```

profile of v0, /device:TPU:0, one launch (start us, length us, event | category | flops | bytes accessed | tf_op | source)
XLA Modules:
  0.0 632.8 jit_solution(8107940526218711960)
XLA Ops:
  8.8 18.2 %fusion.1 = f32[2048,512]{1,0:T(8,128)} fusion(bf16[2048,512]{1,0:T(8,128)(2,1)S(1)} %copy-done, f32[2048,2048]{1,0:T(8,128)} %param.5, bf16[2048,2048]{1,0:T(8,128)(2,1)} %param.6), kind=kOutput, calls=%fused_computation.6 | convolution fusion | flops 25778192384 | bytes 31457280 | tf_op jit(solution)/shard_map/dot_general | solution.py:21
  27.0 159.2 %all-reduce.4.cloned.1.call-done = f32[2048,512]{1,0:T(8,128)} async-done(((f32[2048,512]{1,0:T(8,128)}), f32[2048,512]{1,0:T(8,128)}) %all-reduce.4.cloned.1.call-update) | async-done | bytes 4194320 | tf_op jit(solution)/shard_map/psum | solution.py:22
  186.2 11.4 %fusion.42 = f32[512,512]{0,1:T(8,128)} fusion(f32[2048,512]{1,0:T(8,128)} %all-reduce.4.cloned.1.call-done), kind=kOutput, calls=%fused_computation.81 | convolution fusion | flops 6442450944 | bytes 5242880 | tf_op jit(solution)/shard_map/dot_general | solution.py:23
  197.9 35.2 %all-reduce.6.cloned.1.call-done = f32[512,512]{0,1:T(8,128)} async-done(((f32[512,512]{0,1:T(8,128)}), f32[512,512]{0,1:T(8,128)}) %all-reduce.6.cloned.1.call-update) | async-done | bytes 1048592 | tf_op jit(solution)/shard_map/psum | solution.py:23
  236.1 11.7 %cholesky.104 = f32[128,128]{1,0:T(8,128)S(1)} custom-call(f32[128,128]{1,0:T(8,128)S(1)} %cholesky.266), custom_call_target="Cholesky" | custom-call | tf_op jit(solution)/shard_map/jit(cholesky)/cholesky | solution.py:14
  247.9 9.8 %custom-call.31 = f32[1,128,128]{1,2,0:T(8,128)S(1)} custom-call(f32[1,128,128]{2,1,0:T(8,128)S(1)} %get-tuple-element.30), custom_call_target="InvertDiagBlocksLowerTriangular" | custom-call | tf_op jit(solution)/shard_map/jit(cholesky)/cholesky | solution.py:14
  258.5 11.7 %cholesky.217 = f32[128,128]{1,0:T(8,128)S(1)} custom-call(f32[128,128]{1,0:T(8,128)S(1)} %cholesky.270), custom_call_target="Cholesky" | custom-call | tf_op jit(solution)/shard_map/jit(cholesky)/cholesky | solution.py:14
  270.2 10.2 %custom-call.32 = f32[1,128,128]{1,2,0:T(8,128)S(1)} custom-call(f32[1,128,128]{2,1,0:T(8,128)S(1)} %get-tuple-element.27), custom_call_target="InvertDiagBlocksLowerTriangular" | custom-call | tf_op jit(solution)/shard_map/jit(cholesky)/cholesky | solution.py:14
  281.1 11.7 %cholesky.238 = f32[128,128]{1,0:T(8,128)S(1)} custom-call(f32[128,128]{1,0:T(8,128)S(1)} %cholesky.275), custom_call_target="Cholesky" | custom-call | tf_op jit(solution)/shard_map/jit(cholesky)/cholesky | solution.py:14
  293.5 9.8 %custom-call.33 = f32[1,128,128]{1,2,0:T(8,128)S(1)} custom-call(f32[1,128,128]{2,1,0:T(8,128)S(1)} %get-tuple-element.24), custom_call_target="InvertDiagBlocksLowerTriangular" | custom-call | tf_op jit(solution)/shard_map/jit(cholesky)/cholesky | solution.py:14
  303.9 11.7 %cholesky.255 = f32[128,128]{1,0:T(8,128)S(1)} custom-call(f32[128,128]{1,0:T(8,128)S(1)} %convolution_subtract_fusion.4), custom_call_target="Cholesky" | custom-call | tf_op jit(solution)/shard_map/jit(cholesky)/cholesky | solution.py:14
  319.8 8.0 %while.1 = (s32[]{:T(128)}, f32[512,512]{1,0:T(8,128)S(1)}, s32[4,2]{0,1:T(2,128)S(1)}, f32[4,128,128]{2,1,0:T(8,128)S(1)}, s32[]{:T(128)}) while((s32[]{:T(128)}, f32[512,512]{1,0:T(8,128)S(1)}, s32[4,2]{0,1:T(2,128)S(1)}, f32[4,128,128]{2,1,0:T(8,128)S(1)}, s32[]{:T(128)}) %tuple.31), condition=%wide.while_cond, body=%wide.while_body.sunk | while | flops 2 | bytes 131181 | solution.py:15
  327.9 39.3 %custom-call.34 = f32[4,128,128]{1,2,0:T(8,128)S(1)} custom-call(f32[4,128,128]{2,1,0:T(8,128)S(1)} %get-tuple-element.10), custom_call_target="InvertDiagBlocksLowerTriangular" | custom-call | tf_op jit(solution)/shard_map/jit(_solve_triangular)/triangular_solve | solution.py:15
  367.2 2.4 fusion.16
  369.6 3.1 convolution_subtract_fusion.1
  373.8 5.0 convolution_subtract_fusion
  379.9 7.2 %fusion.9 = f32[128,2048]{0,1:T(8,128)S(1)} fusion(f32[128,2048]{1,0:T(8,128)S(1)} %fusion.28, f32[128,2048]{1,0:T(8,128)S(1)} %fusion.30, f32[128,2048]{1,0:T(8,128)S(1)} %fusion.16, f32[512,2048]{0,1:T(8,128)S(1)} %bitcast.57, f32[512,512]{1,0:T(8,128)} %copy-done.7), kind=kOutput, calls=%fused_computation.15 | convolution fusion | flops 1209794560 | bytes 5439488 | tf_op jit(solution)/shard_map/jit(_solve_triangular)/triangular_solve | solution.py:15
  389.2 56.3 %fusion = f32[2048,512]{1,0:T(8,128)} fusion(f32[2048,2048]{1,0:T(8,128)} %param.5, bf16[2048,2048]{1,0:T(8,128)(2,1)S(1)} %bitcast.59, f32[128,2048]{1,0:T(8,128)S(1)} %fusion.27, f32[128,2048]{1,0:T(8,128)S(1)} %fusion.28, f32[128,2048]{1,0:T(8,128)S(1)} %fusion.30, f32[128,2048]{1,0:T(8,128)S(1)} %fusion.16), kind=kOutput, calls=%fused_computation.5 | convolution fusion | flops 25781338112 | bytes 33554432 | tf_op jit(solution)/shard_map/dot_general | solution.py:26
  445.6 45.2 %reduce-scatter.2.cloned.1.call-done = f32[512,512]{1,0:T(8,128)} async-done(((f32[2048,512]{1,0:T(8,128)}), f32[512,512]{1,0:T(8,128)}) %reduce-scatter.2.cloned.1.call-update) | async-done | bytes 1048592 | tf_op jit(solution)/shard_map/reduce_scatter | solution.py:25
  492.1 39.3 %psum.23 = f32[512]{0:T(512)S(1)} all-reduce(f32[512]{0:T(512)S(1)} %multiply_reduce_fusion), channel_id=1, replica_groups=mesh['row'=4,'col'=8] {'row','col'}, use_global_device_ids=true, to_apply=%region_12.13 | all-reduce | flops 512 | bytes 4096 | tf_op jit(solution)/shard_map/psum | solution.py:28
  531.4 2.1 divide_convert_fusion
  533.6 23.5 %all-gather.2.cloned.1.call-done = bf16[2048,512]{1,0:T(8,128)(2,1)} async-done(((bf16[512,512]{1,0:T(8,128)(2,1)}), bf16[2048,512]{1,0:T(8,128)(2,1)}) %all-gather.2.cloned.1.call-update) | async-done | bytes 2097168 | tf_op jit(solution)/shard_map/all_gather | solution.py:31
  557.1 35.6 %multiply_subtract_fusion = f32[2048,2048]{1,0:T(8,128)} fusion(bf16[2048,512]{1,0:T(8,128)(2,1)} %all-gather.2.cloned.1.call-done, f32[2048,2048]{1,0:T(8,128)} %param.5, bf16[2048,2048]{1,0:T(8,128)(2,1)} %param.6, f32[512]{0:T(512)S(1)} %add_sqrt_fusion, f32[128,2048]{1,0:T(8,128)} %copy-done.6, f32[128,2048]{1,0:T(8,128)S(1)} %fusion.28, ...), kind=kOutput, calls=%fused_computation.2 | convolution fusion | flops 25790775296 | bytes 48236544 | tf_op jit(solution)/shard_map/dot_general | solution.py:33
  592.7 32.0 %subtract_convert_fusion = bf16[2048,2048]{1,0:T(8,128)(2,1)} fusion(bf16[2048,2048]{1,0:T(8,128)(2,1)} %param.4, bf16[2048,512]{1,0:T(8,128)(2,1)} %all-gather.2.cloned.1.call-done, f32[128,2048]{1,0:T(8,128)} %copy-done.6, f32[128,2048]{1,0:T(8,128)} %copy-done.4, f32[128,2048]{1,0:T(8,128)} %copy-done.3, f32[128,2048]{1,0:T(8,128)S(1)} %fusion.16), kind=kOutput, calls=%fused_computation.3 | convolution fusion | flops 25789726720 | bytes 23068672 | tf_op jit(solution)/shard_map/dot_general | solution.py:36
  (70 shorter events, 24.2 us)
Async XLA Ops:
  7.2 1.6 copy-start
  7.2 179.1 %all-reduce.4.cloned.1.call-start = ((), (), s32[]{:S(2)}) async-start(), calls=%async_computation.1 | async-start | bytes 8388608 | tf_op jit(solution)/shard_map/psum | solution.py:22
  27.0 206.1 %all-reduce.6.cloned.1.call-start = ((), (), s32[]{:S(2)}) async-start(), calls=%async_computation.2 | async-start | bytes 2097152 | tf_op jit(solution)/shard_map/psum | solution.py:23
  197.7 293.1 %reduce-scatter.2.cloned.1.call-start = ((), (), s32[]{:S(2)}) async-start(), calls=%async_computation.3 | async-start | bytes 5242880 | tf_op jit(solution)/shard_map/reduce_scatter | solution.py:25
  327.8 39.3 %copy-start.7 = (f32[512,512]{1,0:T(8,128)}, f32[512,512]{1,0:T(8,128)S(1)}, u32[]{:S(2)}) copy-start(f32[512,512]{1,0:T(8,128)S(1)} %get-tuple-element.99) | copy-start | bytes 3145732
  367.2 6.6 %copy-start.2 = (f32[2048,512]{1,0:T(8,128)S(1)}, f32[2048,512]{1,0:T(8,128)}, u32[]{:S(2)}) copy-start(f32[2048,512]{1,0:T(8,128)} %all-reduce.4.cloned.1.call-done) | copy-start | bytes 12582916
  372.7 16.5 %slice-start = ((s8[8388608]{0:T(1024)(128)(4,1)}), s8[4194304]{0:T(1024)(128)(4,1)S(1)}, s32[]{:S(2)}) async-start(s8[8388608]{0:T(1024)(128)(4,1)} %bitcast.58), calls=%async_computation.5 | async-start | bytes 8388608
  373.8 183.2 %copy-start.3 = (f32[128,2048]{1,0:T(8,128)}, f32[128,2048]{1,0:T(8,128)S(1)}, u32[]{:S(2)}) copy-start(f32[128,2048]{1,0:T(8,128)S(1)} %fusion.30) | copy-start | bytes 3145732
  378.8 10.4 %slice-start.1 = ((s8[8388608]{0:T(1024)(128)(4,1)}), s8[4194304]{0:T(1024)(128)(4,1)S(1)}, s32[]{:S(2)}) async-start(s8[8388608]{0:T(1024)(128)(4,1)} %bitcast.58), calls=%async_computation.6 | async-start | bytes 8388608
  379.9 177.2 %copy-start.4 = (f32[128,2048]{1,0:T(8,128)}, f32[128,2048]{1,0:T(8,128)S(1)}, u32[]{:S(2)}) copy-start(f32[128,2048]{1,0:T(8,128)S(1)} %fusion.28) | copy-start | bytes 3145732
  388.2 1.0 copy-start.6
  445.6 111.5 %all-gather.2.cloned.1.call-start = ((), (), s32[]{:S(2)}) async-start(), calls=%async_computation.4 | async-start | bytes 2621440 | tf_op jit(solution)/shard_map/all_gather | solution.py:31
  592.7 32.1 %copy-start.5 = (bf16[2048,512]{1,0:T(8,128)(2,1)S(1)}, bf16[2048,512]{1,0:T(8,128)(2,1)}, u32[]{:S(2)}) copy-start(bf16[2048,512]{1,0:T(8,128)(2,1)} %all-gather.2.cloned.1.call-done) | copy-start | bytes 6291460
  592.7 33.4 %copy-start.1 = (bf16[2048,512]{1,0:T(8,128)(2,1)S(1)}, bf16[2048,512]{1,0:T(8,128)(2,1)}, u32[]{:S(2)}) copy-start(bf16[2048,512]{1,0:T(8,128)(2,1)} %param.7) | copy-start | bytes 6291460
Sparse Core Ops, SparseCore 0:
  27.1 159.1 all-reduce.3
  197.8 35.2 all-reduce.5
  445.7 45.0 reduce-scatter.1
  533.7 23.3 all-gather.1
where the time goes:
time: 639 us; the launch traced here: 633 us
  waiting for transfers between devices  263 us (41%)
  matrix products  176 us (28%)
  other arithmetic  123 us (19%)
  blocking collectives  39.3 us (6%)
  between operations  16.8 us (3%)
  local copies, waits for them, and re-layouts  13.5 us (2%)
    psum x1, waiting for transfers between devices, per_device(): left_factor = lax.psum(partial_left, 'col')  159 us
    another operation x14, other arithmetic, orthogonalize(): lower_tri = jnp.linalg.cholesky(gram_matrix)  78.8 us
    dot_general x1, matrix products, per_device(): jnp.dot(buffer.T, orthonormal, precision=high)  56.3 us
    reduce_scatter x1, waiting for transfers between devices, per_device(): lax.psum_scatter(jnp.dot(buffer.T, orthonormal, precision=high), 'row', s...  45.2 us
    another operation x3, other arithmetic, orthogonalize(): jax.scipy.linalg.solve_triangular(lower_tri, left_factor.T, lower=True)  39.6 us
    psum x1, blocking collectives, per_device(): lax.psum(jnp.sum(right_piece * right_piece, axis=0), ('row', 'col'))  39.3 us
    dot_general x1, matrix products, per_device(): jnp.dot(orthonormal * column_scale, basis_float.T, precision=high)  35.6 us
    psum x1, waiting for transfers between devices, per_device(): lax.psum(jnp.dot(left_factor.T, left_factor, precision=high), 'row')  35.2 us
  transfers between devices with their start and end apart: 4, of which 4 were waited for; matrix products, arithmetic and copies ran while one was open for 0% of the time, Pallas kernels for 0%

commit v1 on v0

--- a/solution.py
+++ b/solution.py
@@ -8,6 +8,23 @@
 decay_loss = 0.1
 step_size = 0.4
 epsilon = 1e-06
+
+
+def in_order(blocks, dim):
+    blocks = jnp.moveaxis(blocks, 0, dim)
+    dims = blocks.shape
+    return blocks.reshape(*dims[:dim], dims[dim] * dims[dim + 1], *dims[dim + 2 :])
+
+
+def doubled(x, axis):
+    size, index = (lax.axis_size(axis), lax.axis_index(axis))
+    parts, distance = (x[None], 1)
+    while distance < size:
+        other = lax.ppermute(parts, axis, [(i, i ^ distance) for i in range(size)])
+        low = index & distance == 0
+        parts = jnp.concatenate([jnp.where(low, parts, other), jnp.where(low, other, parts)])
+        distance *= 2
+    return parts
 
 
 def orthogonalize(left_factor, gram_matrix):
@@ -28,7 +45,7 @@
     square_sum = lax.psum(jnp.sum(right_piece * right_piece, axis=0), ("row", "col"))
     column_scale = jnp.sqrt(square_sum / N + epsilon)
     basis_piece = (right_piece / column_scale).astype(jnp.bfloat16)
-    new_basis = lax.all_gather(basis_piece, "row", axis=0, tiled=True)
+    new_basis = in_order(doubled(basis_piece, "row"), 0)
     basis_float = new_basis.astype(jnp.float32)
     new_momentum = buffer - decay_loss * jnp.dot(
         orthonormal * column_scale, basis_float.T, precision=high

time: 639 us -> 649 us (1.016)
    ppermute x0 -> x2, waiting for transfers between devices: none -> 26 us  [doubled(): other = lax.ppermute(parts, axis, [(i, i ^ distance) for i in range(size)])]
    all_gather x1 -> x0, waiting for transfers between devices: 23.5 us -> none  [per_device(): new_basis = lax.all_gather(basis_piece, 'row', axis=0, tiled=True)]
  transfers between devices with their start and end apart: 4 -> 5, of which waited for: 4 -> 5; matrix products, arithmetic and copies ran while one was open for 0% -> 0% of each run, Pallas kernels for 0% -> 0%
where the time goes in v1:
time: 649 us; the launch traced here: 643 us
  waiting for transfers between devices  266 us (41%)
  matrix products  176 us (27%)
  other arithmetic  129 us (20%)
  blocking collectives  39.3 us (6%)
  between operations  16.8 us (3%)
  local copies, waits for them, and re-layouts  13 us (2%)
    psum x1, waiting for transfers between devices, per_device(): left_factor = lax.psum(partial_left, 'col')  159 us
    another operation x14, other arithmetic, orthogonalize(): lower_tri = jnp.linalg.cholesky(gram_matrix)  78.8 us
    dot_general x1, matrix products, per_device(): jnp.dot(buffer.T, orthonormal, precision=high)  56.7 us
    reduce_scatter x1, waiting for transfers between devices, per_device(): lax.psum_scatter(jnp.dot(buffer.T, orthonormal, precision=high), 'row', s...  45.2 us
    another operation x3, other arithmetic, orthogonalize(): jax.scipy.linalg.solve_triangular(lower_tri, left_factor.T, lower=True)  39.6 us
    psum x1, blocking collectives, per_device(): lax.psum(jnp.sum(right_piece * right_piece, axis=0), ('row', 'col'))  39.3 us
    dot_general x1, matrix products, per_device(): jnp.dot(orthonormal * column_scale, basis_float.T, precision=high)  35.6 us
    psum x1, waiting for transfers between devices, per_device(): lax.psum(jnp.dot(left_factor.T, left_factor, precision=high), 'row')  35.2 us
  transfers between devices with their start and end apart: 5, of which 5 were waited for; matrix products, arithmetic and copies ran while one was open for 0% of the time, Pallas kernels for 0%

profile of v1, /device:TPU:0, one launch (start us, length us, event | category | flops | bytes accessed | tf_op | source)
XLA Modules:
  0.0 642.8 jit_solution(13984277197844494503)
XLA Ops:
  8.8 18.2 %fusion.1 = f32[2048,512]{1,0:T(8,128)} fusion(bf16[2048,512]{1,0:T(8,128)(2,1)S(1)} %copy-done, f32[2048,2048]{1,0:T(8,128)} %param.5, bf16[2048,2048]{1,0:T(8,128)(2,1)} %param.6), kind=kOutput, calls=%fused_computation.6 | convolution fusion | flops 25778192384 | bytes 31457280 | tf_op jit(solution)/shard_map/dot_general | solution.py:38
  27.0 159.2 %all-reduce.4.cloned.1.call-done = f32[2048,512]{1,0:T(8,128)} async-done(((f32[2048,512]{1,0:T(8,128)}), f32[2048,512]{1,0:T(8,128)}) %all-reduce.4.cloned.1.call-update) | async-done | bytes 4194320 | tf_op jit(solution)/shard_map/psum | solution.py:39
  186.2 11.4 %fusion.43 = f32[512,512]{0,1:T(8,128)} fusion(f32[2048,512]{1,0:T(8,128)} %all-reduce.4.cloned.1.call-done), kind=kOutput, calls=%fused_computation.88 | convolution fusion | flops 6442450944 | bytes 5242880 | tf_op jit(solution)/shard_map/dot_general | solution.py:40
  197.9 35.2 %all-reduce.6.cloned.1.call-done = f32[512,512]{0,1:T(8,128)} async-done(((f32[512,512]{0,1:T(8,128)}), f32[512,512]{0,1:T(8,128)}) %all-reduce.6.cloned.1.call-update) | async-done | bytes 1048592 | tf_op jit(solution)/shard_map/psum | solution.py:40
  236.1 11.7 %cholesky.104 = f32[128,128]{1,0:T(8,128)S(1)} custom-call(f32[128,128]{1,0:T(8,128)S(1)} %cholesky.266), custom_call_target="Cholesky" | custom-call | tf_op jit(solution)/shard_map/jit(cholesky)/cholesky | solution.py:31
  247.9 9.8 %custom-call.31 = f32[1,128,128]{1,2,0:T(8,128)S(1)} custom-call(f32[1,128,128]{2,1,0:T(8,128)S(1)} %get-tuple-element.34), custom_call_target="InvertDiagBlocksLowerTriangular" | custom-call | tf_op jit(solution)/shard_map/jit(cholesky)/cholesky | solution.py:31
  258.5 11.7 %cholesky.217 = f32[128,128]{1,0:T(8,128)S(1)} custom-call(f32[128,128]{1,0:T(8,128)S(1)} %cholesky.270), custom_call_target="Cholesky" | custom-call | tf_op jit(solution)/shard_map/jit(cholesky)/cholesky | solution.py:31
  270.2 10.2 %custom-call.32 = f32[1,128,128]{1,2,0:T(8,128)S(1)} custom-call(f32[1,128,128]{2,1,0:T(8,128)S(1)} %get-tuple-element.31), custom_call_target="InvertDiagBlocksLowerTriangular" | custom-call | tf_op jit(solution)/shard_map/jit(cholesky)/cholesky | solution.py:31
  281.1 11.7 %cholesky.238 = f32[128,128]{1,0:T(8,128)S(1)} custom-call(f32[128,128]{1,0:T(8,128)S(1)} %cholesky.275), custom_call_target="Cholesky" | custom-call | tf_op jit(solution)/shard_map/jit(cholesky)/cholesky | solution.py:31
  293.5 9.8 %custom-call.33 = f32[1,128,128]{1,2,0:T(8,128)S(1)} custom-call(f32[1,128,128]{2,1,0:T(8,128)S(1)} %get-tuple-element.28), custom_call_target="InvertDiagBlocksLowerTriangular" | custom-call | tf_op jit(solution)/shard_map/jit(cholesky)/cholesky | solution.py:31
  303.9 11.7 %cholesky.255 = f32[128,128]{1,0:T(8,128)S(1)} custom-call(f32[128,128]{1,0:T(8,128)S(1)} %convolution_subtract_fusion.4), custom_call_target="Cholesky" | custom-call | tf_op jit(solution)/shard_map/jit(cholesky)/cholesky | solution.py:31
  319.8 8.0 %while.1 = (s32[]{:T(128)}, f32[512,512]{1,0:T(8,128)S(1)}, s32[4,2]{0,1:T(2,128)S(1)}, f32[4,128,128]{2,1,0:T(8,128)S(1)}, s32[]{:T(128)}) while((s32[]{:T(128)}, f32[512,512]{1,0:T(8,128)S(1)}, s32[4,2]{0,1:T(2,128)S(1)}, f32[4,128,128]{2,1,0:T(8,128)S(1)}, s32[]{:T(128)}) %tuple.33), condition=%wide.while_cond, body=%wide.while_body.sunk | while | flops 2 | bytes 131181 | solution.py:32
  327.9 39.3 %custom-call.34 = f32[4,128,128]{1,2,0:T(8,128)S(1)} custom-call(f32[4,128,128]{2,1,0:T(8,128)S(1)} %get-tuple-element.10), custom_call_target="InvertDiagBlocksLowerTriangular" | custom-call | tf_op jit(solution)/shard_map/jit(_solve_triangular)/triangular_solve | solution.py:32
  367.2 2.4 fusion.16
  369.6 3.1 convolution_subtract_fusion.1
  373.8 5.0 convolution_subtract_fusion
  379.9 6.8 %fusion.9 = f32[128,2048]{0,1:T(8,128)S(1)} fusion(f32[128,2048]{1,0:T(8,128)S(1)} %fusion.29, f32[128,2048]{1,0:T(8,128)S(1)} %fusion.31, f32[128,2048]{1,0:T(8,128)S(1)} %fusion.16, f32[512,2048]{0,1:T(8,128)S(1)} %bitcast.62, f32[512,512]{1,0:T(8,128)} %copy-done.8), kind=kOutput, calls=%fused_computation.15 | convolution fusion | flops 1209794560 | bytes 5439488 | tf_op jit(solution)/shard_map/jit(_solve_triangular)/triangular_solve | solution.py:32
  388.8 56.7 %fusion = f32[2048,512]{1,0:T(8,128)} fusion(f32[2048,2048]{1,0:T(8,128)} %param.5, bf16[2048,2048]{1,0:T(8,128)(2,1)S(1)} %bitcast.64, f32[128,2048]{1,0:T(8,128)S(1)} %fusion.28, f32[128,2048]{1,0:T(8,128)S(1)} %fusion.29, f32[128,2048]{1,0:T(8,128)S(1)} %fusion.31, f32[128,2048]{1,0:T(8,128)S(1)} %fusion.16), kind=kOutput, calls=%fused_computation.5 | convolution fusion | flops 25781338112 | bytes 33554432 | tf_op jit(solution)/shard_map/dot_general | solution.py:43
  445.6 45.2 %reduce-scatter.2.cloned.1.call-done = f32[512,512]{1,0:T(8,128)} async-done(((f32[2048,512]{1,0:T(8,128)}), f32[512,512]{1,0:T(8,128)}) %reduce-scatter.2.cloned.1.call-update) | async-done | bytes 1048592 | tf_op jit(solution)/shard_map/reduce_scatter | solution.py:42
  492.1 39.3 %psum.23 = f32[512]{0:T(512)S(1)} all-reduce(f32[512]{0:T(512)S(1)} %multiply_reduce_fusion), channel_id=1, replica_groups=mesh['row'=4,'col'=8] {'row','col'}, use_global_device_ids=true, to_apply=%region_12.13 | all-reduce | flops 512 | bytes 4096 | tf_op jit(solution)/shard_map/psum | solution.py:45
  539.2 2.3 collective-permute-start.1
  541.4 23.8 %collective-permute-done.1 = bf16[2,512,512]{2,1,0:T(8,128)(2,1)} collective-permute-done((bf16[2,512,512]{2,1,0:T(8,128)(2,1)}, bf16[2,512,512]{2,1,0:T(8,128)(2,1)}, u32[]{:S(2)}, u32[]{:S(2)}) %collective-permute-start.1) | collective-permute-done | bytes 1048608 | tf_op jit(solution)/shard_map/ppermute | solution.py:23
  568.4 35.6 %multiply_subtract_fusion = f32[2048,2048]{1,0:T(8,128)} fusion(bf16[2048,512]{1,0:T(8,128)(2,1)} %bitcast.65, f32[2048,2048]{1,0:T(8,128)} %param.5, bf16[2048,2048]{1,0:T(8,128)(2,1)} %param.6, f32[512]{0:T(512)S(1)} %add_sqrt_fusion, f32[128,2048]{1,0:T(8,128)} %copy-done.7, f32[128,2048]{1,0:T(8,128)S(1)} %fusion.29, f32[128,2048]{1,0:T(8,128)S(1)} %fusion.31, ...), kind=kOutput, calls=%fused_computation.2 | convolution fusion | flops 25790775296 | bytes 48236544 | tf_op jit(solution)/shard_map/dot_general | solution.py:50
  604.0 32.0 %subtract_convert_fusion = bf16[2048,2048]{1,0:T(8,128)(2,1)} fusion(bf16[2048,2048]{1,0:T(8,128)(2,1)} %param.4, bf16[2048,512]{1,0:T(8,128)(2,1)} %bitcast.66, f32[128,2048]{1,0:T(8,128)} %copy-done.7, f32[128,2048]{1,0:T(8,128)} %copy-done.4, f32[128,2048]{1,0:T(8,128)} %copy-done.3, f32[128,2048]{1,0:T(8,128)S(1)} %fusion.16), kind=kOutput, calls=%fused_computation.3 | convolution fusion | flops 25789726720 | bytes 23068672 | tf_op jit(solution)/shard_map/dot_general | solution.py:53
  (76 shorter events, 33.7 us)
Async XLA Ops:
  7.2 1.6 copy-start
  7.2 179.1 %all-reduce.4.cloned.1.call-start = ((), (), s32[]{:S(2)}) async-start(), calls=%async_computation.1 | async-start | bytes 8388608 | tf_op jit(solution)/shard_map/psum | solution.py:39
  27.0 206.1 %all-reduce.6.cloned.1.call-start = ((), (), s32[]{:S(2)}) async-start(), calls=%async_computation.2 | async-start | bytes 2097152 | tf_op jit(solution)/shard_map/psum | solution.py:40
  197.7 293.1 %reduce-scatter.2.cloned.1.call-start = ((), (), s32[]{:S(2)}) async-start(), calls=%async_computation.3 | async-start | bytes 5242880 | tf_op jit(solution)/shard_map/reduce_scatter | solution.py:42
  327.8 39.3 %copy-start.8 = (f32[512,512]{1,0:T(8,128)}, f32[512,512]{1,0:T(8,128)S(1)}, u32[]{:S(2)}) copy-start(f32[512,512]{1,0:T(8,128)S(1)} %get-tuple-element.95) | copy-start | bytes 3145732
  367.2 6.6 %copy-start.2 = (f32[2048,512]{1,0:T(8,128)S(1)}, f32[2048,512]{1,0:T(8,128)}, u32[]{:S(2)}) copy-start(f32[2048,512]{1,0:T(8,128)} %all-reduce.4.cloned.1.call-done) | copy-start | bytes 12582916
  372.7 16.1 %slice-start = ((s8[8388608]{0:T(1024)(128)(4,1)}), s8[4194304]{0:T(1024)(128)(4,1)S(1)}, s32[]{:S(2)}) async-start(s8[8388608]{0:T(1024)(128)(4,1)} %bitcast.63), calls=%async_computation.4 | async-start | bytes 8388608
  373.8 194.6 %copy-start.3 = (f32[128,2048]{1,0:T(8,128)}, f32[128,2048]{1,0:T(8,128)S(1)}, u32[]{:S(2)}) copy-start(f32[128,2048]{1,0:T(8,128)S(1)} %fusion.31) | copy-start | bytes 3145732
  378.8 10.0 %slice-start.1 = ((s8[8388608]{0:T(1024)(128)(4,1)}), s8[4194304]{0:T(1024)(128)(4,1)S(1)}, s32[]{:S(2)}) async-start(s8[8388608]{0:T(1024)(128)(4,1)} %bitcast.63), calls=%async_computation.5 | async-start | bytes 8388608
  379.9 188.5 %copy-start.4 = (f32[128,2048]{1,0:T(8,128)}, f32[128,2048]{1,0:T(8,128)S(1)}, u32[]{:S(2)}) copy-start(f32[128,2048]{1,0:T(8,128)S(1)} %fusion.29) | copy-start | bytes 3145732
  387.8 1.0 copy-start.7
  533.6 2.3 collective-permute-start
  537.3 0.8 copy-start.5
  537.3 1.8 copy-start.6
  539.2 26.0 %collective-permute-start.1 = (bf16[2,512,512]{2,1,0:T(8,128)(2,1)}, bf16[2,512,512]{2,1,0:T(8,128)(2,1)}, u32[]{:S(2)}, u32[]{:S(2)}) collective-permute-start(bf16[2,512,512]{2,1,0:T(8,128)(2,1)} %pad_maximum_fusion.2), channel_id=1, source_target_pairs={{0,16},{8,24},{16,0},{24,8},{1,17},{9,25},{17,1},{25,9},{2,18},{10... | collective-permute-start | bytes 3145736 | tf_op jit(solution)/shard_map/ppermute | solution.py:23
  604.0 32.0 %copy-start.1 = (bf16[2048,512]{1,0:T(8,128)(2,1)S(1)}, bf16[2048,512]{1,0:T(8,128)(2,1)}, u32[]{:S(2)}) copy-start(bf16[2048,512]{1,0:T(8,128)(2,1)} %param.7) | copy-start | bytes 6291460
Sparse Core Ops, SparseCore 0:
  27.1 159.1 all-reduce.3
  197.8 35.2 all-reduce.5
  445.7 45.0 reduce-scatter.1
